TPU v7x, 32 devices: a whole 2x2x4 slice. The times are simulated.
32 devices in a mesh: parts: 2 (over y), space: 4 (over z), filt: 2 (over x), rep: 2 (over core).
Axes of the slice: x: 2, y: 2, z: 4, core: 2. Of those that a mesh axis runs over, the one named last changes fastest.
Arguments:
- features: bfloat16 [128, 512, 256], P(('parts', 'space'), 'filt', 'rep'), parts along dimension 0, may hold values from -6 to 6
- kernel: bfloat16 [3, 3, 512, 512], P(None, None, 'filt'), may hold values from -0.09375 to 0.09375
- shift_bias: float32 [512], P('filt'), may hold values from -3 to 3
- upstream: bfloat16 [128, 512, 256], P(('parts', 'space'), 'filt', 'rep'), parts along dimension 0, may hold values from -6 to 6
Outputs:
- block_out: bfloat16 [128, 512, 256], P(('parts', 'space'), 'filt', 'rep'), parts along dimension 0
- input_grad: bfloat16 [128, 512, 256], P(('parts', 'space'), 'filt', 'rep'), parts along dimension 0
- kernel_grad: float32 [6, 3, 512, 512], P('parts', None, 'filt'), parts along dimension 0
- bias_grad: float32 [1024], P(('parts', 'filt')), parts along dimension 0
There are 2 independent parts, one for each index of `parts`. A program takes and returns all parts, laid end to end along the dimension named above; an argument that names none is the same for every part. Nothing has to cross between parts.
All inputs are finite; a program needn't handle non-finite values.
Results may differ from a plain program's by a relative error of at most 0.0055.
Values may be sent and summed in bfloat16 or wider, within the bound.
No kernel may reach another device: no remote copies, remote signals or barrier semaphores. Data moves between devices by JAX's collectives and lax.ppermute only.
A program may use at most 64 MiB of HBM per device.

v0:
```python
import jax
import jax.numpy as jnp
from jax import lax
from jax.sharding import PartitionSpec as P


def padded(cells, sides, width):
    for axis, dim in sides:
        count = lax.axis_size(axis)
        ends = count - 1
        head = lax.slice_in_dim(cells, 0, width, axis=dim)
        tail = lax.slice_in_dim(cells, cells.shape[dim] - width, cells.shape[dim], axis=dim)
        cells = jnp.concatenate(
            [
                lax.ppermute(tail, axis, [(i, (i + 1) % count) for i in range(ends)]),
                cells,
                lax.ppermute(head, axis, [((i + 1) % count, i) for i in range(ends)]),
            ],
            axis=dim,
        )
    return cells


def forward_taps(running, panels, kernel, band_rows, band_cols):
    for row_tap in range(3):
        for col_tap in range(3):
            window = panels[row_tap : row_tap + band_rows, :, col_tap : col_tap + band_cols]
            weights = kernel[row_tap, col_tap]
            running = running + jnp.einsum(
                "oc,hcw->how", weights, window, preferred_element_type=jnp.float32
            )
    return running


def weight_taps(panels, slope, band_rows, band_cols):
    rows_out = []
    for row_tap in range(3):
        taps_row = []
        for col_tap in range(3):
            window = panels[row_tap : row_tap + band_rows, :, col_tap : col_tap + band_cols]
            taps_row.append(
                jnp.einsum("how,hcw->oc", slope, window, preferred_element_type=jnp.float32)
            )
        rows_out.append(jnp.stack(taps_row))
    return jnp.stack(rows_out)


def backward_taps(slope_pad, weights, band_rows, band_cols):
    summed = jnp.zeros((band_rows, weights.shape[3], band_cols), jnp.float32)
    for row_tap in range(3):
        for col_tap in range(3):
            part_slope = slope_pad[
                2 - row_tap : 2 - row_tap + band_rows, :, 2 - col_tap : 2 - col_tap + band_cols
            ]
            summed = summed + jnp.einsum(
                "oc,how->hcw",
                weights[row_tap, col_tap],
                part_slope,
                preferred_element_type=jnp.float32,
            )
    return summed


def per_device(features, kernel, shift_bias, upstream):
    band_rows, local_out, band_cols = upstream.shape
    rimmed = padded(features, (("space", 0), ("rep", 2)), 1)
    start_pre = (
        jnp.zeros((band_rows, local_out, band_cols), jnp.float32) + shift_bias[None, :, None]
    )
    all_panels = lax.all_gather(rimmed, "filt", axis=1, tiled=True)
    pre = forward_taps(start_pre, all_panels, kernel, band_rows, band_cols)
    sigm = jax.nn.sigmoid(pre)
    block_out = (features.astype(jnp.float32) + pre * sigm).astype(jnp.bfloat16)
    slope = (upstream.astype(jnp.float32) * sigm * (1.0 + pre * (1.0 - sigm))).astype(jnp.bfloat16)
    kernel_part = weight_taps(all_panels, slope, band_rows, band_cols)
    slope_pad = padded(slope, (("space", 0), ("rep", 2)), 1)
    slope_all = lax.all_gather(slope_pad, "filt", axis=1, tiled=True)
    own_rows = lax.all_to_all(kernel, "filt", split_axis=3, concat_axis=2, tiled=True)
    back = backward_taps(slope_all, own_rows, band_rows, band_cols)
    input_grad = (upstream.astype(jnp.float32) + back).astype(jnp.bfloat16)
    bias_part = jnp.sum(slope.astype(jnp.float32), axis=(0, 2))
    kernel_sum, bias_sum = lax.psum((kernel_part, bias_part), ("space", "rep"))
    total_cells = band_rows * band_cols * lax.axis_size("space") * lax.axis_size("rep")
    scale = 1.0 / jnp.sqrt(jnp.float32(total_cells))
    return (block_out, input_grad, kernel_sum * scale, bias_sum * scale)


def solution(mesh):
    in_specs = (
        P(("parts", "space"), "filt", "rep"),
        P(None, None, "filt", None),
        P("filt"),
        P(("parts", "space"), "filt", "rep"),
    )
    out_specs = (
        P(("parts", "space"), "filt", "rep"),
        P(("parts", "space"), "filt", "rep"),
        P("parts", None, "filt", None),
        P(("parts", "filt")),
    )
    return jax.shard_map(
        per_device, mesh=mesh, in_specs=in_specs, out_specs=out_specs, check_vma=False
    )
```

profile of v0, /device:TPU:0, one launch (start us, length us, event | category | flops | bytes accessed | tf_op | source)
XLA Modules:
  0.0 250.9 jit_solution(6216047578776951642)
XLA Ops:
  7.2 0.0 all-gather.3.cloned.1.call-start
  7.2 1.5 copy.34
  8.7 1.3 collective-permute-start.1
  10.0 5.6 %collective-permute-start = (bf16[1,256,128]{1,2,0:T(8,128)(2,1)S(1)}, bf16[1,256,128]{1,2,0:T(8,128)(2,1)S(1)}, u32[]{:S(2)}, u32[]{:S(2)}) collective-permute-start(bf16[1,256,128]{1,2,0:T(8,128)(2,1)S(1)} %get-tuple-element.21), channel_id=1, source_target_pairs={{0,4},{4,8},{8,12},{1,5},{5,9},{9,13},{2,6},{6,10},{10,14},{3,7},{... | collective-permute-start | bytes 196616 | tf_op jit(solution)/shard_map/ppermute | solution.py:15
  15.6 0.3 collective-permute-done.1
  15.9 1.6 collective-permute-done
  17.6 1.4 collective-permute-start.3
  19.0 3.0 %collective-permute-start.2 = (bf16[18,256,1]{1,2,0:T(2,128)(2,1)S(1)}, bf16[18,256,1]{1,2,0:T(2,128)(2,1)S(1)}, u32[]{:S(2)}, u32[]{:S(2)}) collective-permute-start(bf16[18,256,1]{1,2,0:T(2,128)(2,1)S(1)} %get-tuple-element.17), channel_id=1, source_target_pairs={{0,1},{2,3},{4,5},{6,7},{8,9},{10,11},{12,13},{14,15},{16,17},{18,... | collective-permute-start | bytes 27656 | tf_op jit(solution)/shard_map/ppermute | solution.py:15
  22.0 0.8 collective-permute-done.2
  22.8 1.7 pad_maximum_fusion.1
  24.6 0.0 all-reduce.2.cloned.1.call-start
  24.6 0.5 copy.38
  25.2 39.7 %all-gather.3.cloned.1.call-done = bf16[18,512,130]{1,2,0:T(8,128)(2,1)} async-done(((bf16[18,256,130]{1,2,0:T(8,128)(2,1)}), bf16[18,512,130]{1,2,0:T(8,128)(2,1)}) %all-gather.3.cloned.1.call-update) | async-done | bytes 2396176 | tf_op jit(solution)/shard_map/all_gather | solution.py:70
  64.9 2.5 %fusion.33 = f32[16,128,256]{2,1,0:T(8,128)S(1)} fusion(bf16[18,512,130]{1,2,0:T(8,128)(2,1)} %all-gather.3.cloned.1.call-done, bf16[3,3,256,512]{3,2,1,0:T(8,128)(2,1)} %param.5), kind=kOutput, calls=%fused_computation.42 | convolution fusion | flops 536870912 | bytes 4456448 | tf_op jit(solution)/shard_map/oc,hcw->how/dot_general | solution.py:29
  67.4 0.6 copy-done.2
  68.1 0.7 fusion.37
  68.8 0.8 fusion.41
  69.6 0.8 fusion.45
  70.3 0.7 fusion.49
  71.1 0.8 fusion.53
  71.8 0.8 fusion.57
  72.6 0.7 fusion.61
  73.4 3.4 %convert_reduce_fusion = (f32[256]{0:T(256)S(1)}, bf16[16,256,128]{1,2,0:T(8,128)(2,1)S(1)}, bf16[16,256,128]{1,2,0:T(8,128)(2,1)}) fusion(bf16[16,256,128]{1,2,0:T(8,128)(2,1)S(1)} %copy.38, bf16[16,256,128]{1,2,0:T(8,128)(2,1)S(1)} %copy.34, bf16[3,3,256,512]{3,2,1,0:T(8,128)(2,1)S(1)} %copy-done.2, bf16[18,512,130]{1,2,0:T(8,128)(2,1)S(1)} %copy-done, ...), kind=kOutput, calls=%fused_computation.35 | convolution fusion | flops 549977856 | bytes 23332864 | tf_op jit(solution)/shard_map/oc,hcw->how/dot_general | solution.py:29
  76.8 0.8 fusion.91
  77.6 0.8 fusion.88
  78.3 0.7 fusion.85
  79.1 0.1 maximum_bitcast_fusion.2
  79.2 0.8 fusion.73
  80.0 0.8 fusion.70
  80.8 0.7 fusion.67
  81.5 0.8 fusion.82
  82.3 0.8 fusion.79
  83.0 0.7 fusion.76
  83.8 0.6 maximum_bitcast_fusion
  84.3 2.7 %pad_maximum_fusion = f32[3,3,256,512]{3,2,1,0:T(8,128)} fusion(f32[1,3,256,512]{3,2,1,0:T(8,128)S(1)} %maximum_bitcast_fusion.2, f32[1,3,256,512]{3,2,1,0:T(8,128)S(1)} %get-tuple-element.24, f32[1,3,256,512]{3,2,1,0:T(8,128)S(1)} %get-tuple-element.23), kind=kLoop, calls=%fused_computation | loop fusion | flops 2359296 | bytes 9437184 | tf_op jit(solution)/shard_map/stack | solution.py:45
  87.1 0.0 all-gather.5.cloned.1.call-start
  87.1 1.3 collective-permute-start.5
  88.4 4.5 %collective-permute-start.4 = (bf16[1,256,128]{1,2,0:T(8,128)(2,1)S(1)}, bf16[1,256,128]{1,2,0:T(8,128)(2,1)S(1)}, u32[]{:S(2)}, u32[]{:S(2)}) collective-permute-start(bf16[1,256,128]{1,2,0:T(8,128)(2,1)S(1)} %get-tuple-element.19), channel_id=1, source_target_pairs={{0,4},{4,8},{8,12},{1,5},{5,9},{9,13},{2,6},{6,10},{10,14},{3,7},{... | collective-permute-start | bytes 196616 | tf_op jit(solution)/shard_map/ppermute | solution.py:15
  93.0 0.3 collective-permute-done.5
  93.3 3.0 %collective-permute-done.4 = bf16[1,256,128]{1,2,0:T(8,128)(2,1)S(1)} collective-permute-done((bf16[1,256,128]{1,2,0:T(8,128)(2,1)S(1)}, bf16[1,256,128]{1,2,0:T(8,128)(2,1)S(1)}, u32[]{:S(2)}, u32[]{:S(2)}) %collective-permute-start.4) | collective-permute-done | bytes 65568 | tf_op jit(solution)/shard_map/ppermute | solution.py:15
  96.4 1.4 collective-permute-start.7
  97.8 3.0 %collective-permute-start.6 = (bf16[18,256,1]{1,2,0:T(2,128)(2,1)S(1)}, bf16[18,256,1]{1,2,0:T(2,128)(2,1)S(1)}, u32[]{:S(2)}, u32[]{:S(2)}) collective-permute-start(bf16[18,256,1]{1,2,0:T(2,128)(2,1)S(1)} %get-tuple-element.15), channel_id=1, source_target_pairs={{0,1},{2,3},{4,5},{6,7},{8,9},{10,11},{12,13},{14,15},{16,17},{18,... | collective-permute-start | bytes 27656 | tf_op jit(solution)/shard_map/ppermute | solution.py:15
  100.8 0.8 collective-permute-done.6
  101.7 1.7 pad_maximum_fusion.2
  103.4 3.8 %copy.39 = bf16[3,3,256,512]{2,1,0,3:T(4,128)(2,1)} copy(bf16[3,3,256,512]{3,2,1,0:T(8,128)(2,1)S(1)} %copy-done.3) | data formatting | bytes 4718592 | tf_op args[1]
  107.2 40.8 %all_to_all.18 = bf16[3,3,256,512]{2,1,0,3:T(4,128)(2,1)S(1)} all-to-all(bf16[3,3,256,512]{2,1,0,3:T(4,128)(2,1)} %copy.39), channel_id=1, replica_groups=mesh['parts'=2,'space'=4,'filt'=2,'rep'=2] {'filt'}, dimensions={3} | all-to-all | bytes 4718592 | tf_op jit(solution)/shard_map/all_to_all | solution.py:78
  148.0 3.6 %copy.40 = bf16[3,3,256,2,256]{4,2,3,1,0:T(8,128)(2,1)} copy(bf16[3,3,256,2,256]{2,1,0,4,3:T(4,128)(2,1)S(1)} %bitcast.163) | data formatting | bytes 4718592 | tf_op jit(solution)/shard_map/all_to_all | solution.py:78
  151.6 2.3 copy.59
  153.9 17.7 %psum.15 = f32[256]{0:T(256)S(1)} all-reduce(f32[256]{0:T(256)S(1)} %get-tuple-element.12), channel_id=1, replica_groups=mesh['parts'=2,'space'=4,'filt'=2,'rep'=2] {'space','rep'}, use_global_device_ids=true, to_apply=%region_2.0 | all-reduce | flops 256 | bytes 2048 | tf_op jit(solution)/shard_map/psum | solution.py:82
  171.6 0.6 broadcast_multiply_fusion.1
  172.1 22.5 %all-reduce.2.cloned.1.call-done = f32[3,3,256,512]{3,2,1,0:T(8,128)} async-done(((f32[3,3,256,512]{3,2,1,0:T(8,128)}), f32[3,3,256,512]{3,2,1,0:T(8,128)}) %all-reduce.2.cloned.1.call-update) | async-done | bytes 4718608 | tf_op jit(solution)/shard_map/psum | solution.py:82
  194.6 5.3 %broadcast_multiply_fusion = f32[3,3,256,512]{3,2,1,0:T(8,128)} fusion(f32[3,3,256,512]{3,2,1,0:T(8,128)} %all-reduce.2.cloned.1.call-done), kind=kLoop, calls=%fused_computation.3 | loop fusion | flops 1179648 | bytes 9437184 | tf_op jit(solution)/shard_map/mul | solution.py:85
  199.9 34.0 %all-gather.5.cloned.1.call-done = bf16[18,512,130]{1,2,0:T(8,128)(2,1)} async-done(((bf16[18,256,130]{1,2,0:T(8,128)(2,1)}), bf16[18,512,130]{1,2,0:T(8,128)(2,1)}) %all-gather.5.cloned.1.call-update) | async-done | bytes 2396176 | tf_op jit(solution)/shard_map/all_gather | solution.py:77
  233.9 2.5 fusion.5
  236.4 0.7 fusion.7
  237.2 0.7 fusion.9
  237.9 0.7 fusion.11
  238.6 0.7 fusion.13
  239.3 0.7 fusion.15
  240.0 0.7 fusion.19
  240.8 0.7 fusion.17
  241.5 0.5 copy-done.6
  242.0 1.1 fusion.2
  243.1 1.3 copy.60
  (25 shorter events, 0.2 us)
Async XLA Ops:
  7.2 57.7 %all-gather.3.cloned.1.call-start = ((), (), s32[]{:S(2)}) async-start(), calls=%async_computation.1 | async-start | bytes 3760128 | tf_op jit(solution)/shard_map/all_gather | solution.py:70
  8.7 7.2 %collective-permute-start.1 = (bf16[1,256,128]{1,2,0:T(8,128)(2,1)S(1)}, bf16[1,256,128]{1,2,0:T(8,128)(2,1)S(1)}, u32[]{:S(2)}, u32[]{:S(2)}) collective-permute-start(bf16[1,256,128]{1,2,0:T(8,128)(2,1)S(1)} %get-tuple-element.22), channel_id=1, source_target_pairs={{4,0},{8,4},{12,8},{5,1},{9,5},{13,9},{6,2},{10,6},{14,10},{7,3},{... | collective-permute-start | bytes 196616 | tf_op jit(solution)/shard_map/ppermute | solution.py:17
  10.0 7.5 %collective-permute-start = (bf16[1,256,128]{1,2,0:T(8,128)(2,1)S(1)}, bf16[1,256,128]{1,2,0:T(8,128)(2,1)S(1)}, u32[]{:S(2)}, u32[]{:S(2)}) collective-permute-start(bf16[1,256,128]{1,2,0:T(8,128)(2,1)S(1)} %get-tuple-element.21), channel_id=1, source_target_pairs={{0,4},{4,8},{8,12},{1,5},{5,9},{9,13},{2,6},{6,10},{10,14},{3,7},{... | collective-permute-start | bytes 196616 | tf_op jit(solution)/shard_map/ppermute | solution.py:15
  17.5 7.1 %copy-start.7 = (bf16[16,256,128]{2,1,0:T(8,128)(2,1)S(1)}, bf16[16,256,128]{2,1,0:T(8,128)(2,1)}, u32[]{:S(2)}) copy-start(bf16[16,256,128]{2,1,0:T(8,128)(2,1)} %param.7) | copy-start | bytes 3145732
  17.6 4.5 %collective-permute-start.3 = (bf16[18,256,1]{1,2,0:T(2,128)(2,1)S(1)}, bf16[18,256,1]{1,2,0:T(2,128)(2,1)S(1)}, u32[]{:S(2)}, u32[]{:S(2)}) collective-permute-start(bf16[18,256,1]{1,2,0:T(2,128)(2,1)S(1)} %get-tuple-element.18), channel_id=1, source_target_pairs={{1,0},{3,2},{5,4},{7,6},{9,8},{11,10},{13,12},{15,14},{17,16},{19,... | collective-permute-start | bytes 27656 | tf_op jit(solution)/shard_map/ppermute | solution.py:17
  19.0 3.9 %collective-permute-start.2 = (bf16[18,256,1]{1,2,0:T(2,128)(2,1)S(1)}, bf16[18,256,1]{1,2,0:T(2,128)(2,1)S(1)}, u32[]{:S(2)}, u32[]{:S(2)}) collective-permute-start(bf16[18,256,1]{1,2,0:T(2,128)(2,1)S(1)} %get-tuple-element.17), channel_id=1, source_target_pairs={{0,1},{2,3},{4,5},{6,7},{8,9},{10,11},{12,13},{14,15},{16,17},{18,... | collective-permute-start | bytes 27656 | tf_op jit(solution)/shard_map/ppermute | solution.py:15
  24.6 170.0 %all-reduce.2.cloned.1.call-start = ((), (), s32[]{:S(2)}) async-start(), calls=%async_computation.3 | async-start | bytes 9437184 | tf_op jit(solution)/shard_map/psum | solution.py:82
  25.2 48.2 %copy-start.5 = (bf16[16,256,128]{1,2,0:T(8,128)(2,1)}, bf16[16,256,128]{1,2,0:T(8,128)(2,1)S(1)}, u32[]{:S(2)}) copy-start(bf16[16,256,128]{1,2,0:T(8,128)(2,1)S(1)} %copy.38) | copy-start | bytes 3145732
  64.9 2.5 %copy-start = (bf16[18,512,130]{1,2,0:T(8,128)(2,1)S(1)}, bf16[18,512,130]{1,2,0:T(8,128)(2,1)}, u32[]{:S(2)}) copy-start(bf16[18,512,130]{1,2,0:T(8,128)(2,1)} %all-gather.3.cloned.1.call-done) | copy-start | bytes 7188484
  64.9 3.2 %copy-start.2 = (bf16[3,3,256,512]{3,2,1,0:T(8,128)(2,1)S(1)}, bf16[3,3,256,512]{3,2,1,0:T(8,128)(2,1)}, u32[]{:S(2)}) copy-start(bf16[3,3,256,512]{3,2,1,0:T(8,128)(2,1)} %param.5) | copy-start | bytes 7077892
  72.6 0.8 copy-start.8
  87.1 146.9 %all-gather.5.cloned.1.call-start = ((), (), s32[]{:S(2)}) async-start(), calls=%async_computation.2 | async-start | bytes 3760128 | tf_op jit(solution)/shard_map/all_gather | solution.py:77
  87.1 6.2 %collective-permute-start.5 = (bf16[1,256,128]{1,2,0:T(8,128)(2,1)S(1)}, bf16[1,256,128]{1,2,0:T(8,128)(2,1)S(1)}, u32[]{:S(2)}, u32[]{:S(2)}) collective-permute-start(bf16[1,256,128]{1,2,0:T(8,128)(2,1)S(1)} %get-tuple-element.20), channel_id=1, source_target_pairs={{4,0},{8,4},{12,8},{5,1},{9,5},{13,9},{6,2},{10,6},{14,10},{7,3},{... | collective-permute-start | bytes 196616 | tf_op jit(solution)/shard_map/ppermute | solution.py:17
  88.4 7.9 %collective-permute-start.4 = (bf16[1,256,128]{1,2,0:T(8,128)(2,1)S(1)}, bf16[1,256,128]{1,2,0:T(8,128)(2,1)S(1)}, u32[]{:S(2)}, u32[]{:S(2)}) collective-permute-start(bf16[1,256,128]{1,2,0:T(8,128)(2,1)S(1)} %get-tuple-element.19), channel_id=1, source_target_pairs={{0,4},{4,8},{8,12},{1,5},{5,9},{9,13},{2,6},{6,10},{10,14},{3,7},{... | collective-permute-start | bytes 196616 | tf_op jit(solution)/shard_map/ppermute | solution.py:15
  96.4 7.1 %copy-start.3 = (bf16[3,3,256,512]{3,2,1,0:T(8,128)(2,1)S(1)}, bf16[3,3,256,512]{3,2,1,0:T(8,128)(2,1)}, u32[]{:S(2)}) copy-start(bf16[3,3,256,512]{3,2,1,0:T(8,128)(2,1)} %param.5) | copy-start | bytes 7077892
  96.4 4.5 %collective-permute-start.7 = (bf16[18,256,1]{1,2,0:T(2,128)(2,1)S(1)}, bf16[18,256,1]{1,2,0:T(2,128)(2,1)S(1)}, u32[]{:S(2)}, u32[]{:S(2)}) collective-permute-start(bf16[18,256,1]{1,2,0:T(2,128)(2,1)S(1)} %get-tuple-element.16), channel_id=1, source_target_pairs={{1,0},{3,2},{5,4},{7,6},{9,8},{11,10},{13,12},{15,14},{17,16},{19,... | collective-permute-start | bytes 27656 | tf_op jit(solution)/shard_map/ppermute | solution.py:17
  97.8 3.9 %collective-permute-start.6 = (bf16[18,256,1]{1,2,0:T(2,128)(2,1)S(1)}, bf16[18,256,1]{1,2,0:T(2,128)(2,1)S(1)}, u32[]{:S(2)}, u32[]{:S(2)}) collective-permute-start(bf16[18,256,1]{1,2,0:T(2,128)(2,1)S(1)} %get-tuple-element.15), channel_id=1, source_target_pairs={{0,1},{2,3},{4,5},{6,7},{8,9},{10,11},{12,13},{14,15},{16,17},{18,... | collective-permute-start | bytes 27656 | tf_op jit(solution)/shard_map/ppermute | solution.py:15
  172.1 61.8 %copy-start.4 = (bf16[3,3,256,2,256]{4,2,3,1,0:T(8,128)(2,1)S(1)}, bf16[3,3,256,2,256]{4,2,3,1,0:T(8,128)(2,1)}, u32[]{:S(2)}) copy-start(bf16[3,3,256,2,256]{4,2,3,1,0:T(8,128)(2,1)} %copy.40) | copy-start | bytes 7077892
  233.9 2.5 copy-start.1
  240.8 1.2 copy-start.6
Sparse Core Ops, SparseCore 0:
  24.7 40.1 all-gather.2
  87.2 107.3 all-reduce.1
  196.2 37.7 all-gather.4
where the time goes:
time: 251 us
  waiting for transfers between devices  103 us (41%)
  blocking collectives  58.5 us (23%)
  matrix products  26.5 us (11%)
  starting transfers between devices  21.7 us (9%)
  local copies, waits for them, and re-layouts  14.2 us (6%)
  between operations  14.2 us (6%)
  other arithmetic  12.8 us (5%)
    all_to_all x1, blocking collectives, per_device(): lax.all_to_all(kernel, 'filt', split_axis=3, concat_axis=2, tiled=True)  40.8 us
    all_gather x1, waiting for transfers between devices, per_device(): all_panels = lax.all_gather(rimmed, 'filt', axis=1, tiled=True)  39.7 us
    all_gather x1, waiting for transfers between devices, per_device(): slope_all = lax.all_gather(slope_pad, 'filt', axis=1, tiled=True)  34 us
    psum x1, waiting for transfers between devices, per_device(): kernel_sum, bias_sum = lax.psum((kernel_part, bias_part), ('space', 'rep'))  22.5 us
    psum x1, blocking collectives, per_device(): kernel_sum, bias_sum = lax.psum((kernel_part, bias_part), ('space', 'rep'))  17.7 us
    ppermute x4, starting transfers between devices, padded(): lax.ppermute(tail, axis, [(i, (i + 1) % count) for i in range(ends)])  16.2 us
    dot_general x9, matrix products, forward_taps(): jnp.einsum('oc,hcw->how', weights, window, preferred_element_type=jnp.flo...  11.2 us
    unnamed x23, local copies, waits for them, and re-layouts  10.5 us
  transfers between devices with their start and end apart: 11, of which 9 were waited for; matrix products, arithmetic and copies ran while one was open for 7% of the time, Pallas kernels for 0%

commit v1 on v0

--- a/solution.py
+++ b/solution.py
@@ -79,7 +79,7 @@
     back = backward_taps(slope_all, own_rows, band_rows, band_cols)
     input_grad = (upstream.astype(jnp.float32) + back).astype(jnp.bfloat16)
     bias_part = jnp.sum(slope.astype(jnp.float32), axis=(0, 2))
-    kernel_sum, bias_sum = lax.psum((kernel_part, bias_part), ("space", "rep"))
+    kernel_sum, bias_sum = lax.psum(lax.psum((kernel_part, bias_part), "rep"), "space")
     total_cells = band_rows * band_cols * lax.axis_size("space") * lax.axis_size("rep")
     scale = 1.0 / jnp.sqrt(jnp.float32(total_cells))
     return (block_out, input_grad, kernel_sum * scale, bias_sum * scale)

time: 251 us -> 361 us (1.44)
  waiting for transfers between devices: 103 us -> 251 us
  blocking collectives: 58.5 us -> 15.8 us
  starting transfers between devices: 21.7 us -> 26.1 us
    psum x1 -> x2, waiting for transfers between devices: 22.5 us -> 157 us  [the longest x1 151 us: per_device(): lax.psum(lax.psum((kernel_part, bias_part), 'rep'), 'space')]
    all_to_all x0 -> x1, waiting for transfers between devices: none -> 48.8 us  [per_device(): lax.all_to_all(kernel, 'filt', split_axis=3, concat_axis=2, tiled=True)]
    all_to_all x1 -> x0, blocking collectives: 40.8 us -> none  [per_device(): lax.all_to_all(kernel, 'filt', split_axis=3, concat_axis=2, tiled=True)]
    all_gather x1, waiting for transfers between devices: 34 us -> 0.01 us  [per_device(): slope_all = lax.all_gather(slope_pad, 'filt', axis=1, tiled=True)]
    all_to_all x0 -> x1, starting transfers between devices: none -> 4.21 us  [per_device(): lax.all_to_all(kernel, 'filt', split_axis=3, concat_axis=2, tiled=True)]
    psum x1 -> x2, blocking collectives: 17.7 us -> 15.8 us  [the longest x1 13.3 us: per_device(): lax.psum(lax.psum((kernel_part, bias_part), 'rep'), 'space')]
  transfers between devices with their start and end apart: 11 -> 13, of which waited for: 9 -> 10; matrix products, arithmetic and copies ran while one was open for 7% -> 6% of each run, Pallas kernels for 0% -> 0%
where the time goes in v1:
time: 361 us
  waiting for transfers between devices  251 us (70%)
  matrix products  26.5 us (7%)
  starting transfers between devices  26.1 us (7%)
  blocking collectives  15.8 us (4%)
  local copies, waits for them, and re-layouts  14.8 us (4%)
  between operations  14.2 us (4%)
  other arithmetic  12.8 us (4%)
    psum x1, waiting for transfers between devices, per_device(): lax.psum(lax.psum((kernel_part, bias_part), 'rep'), 'space')  151 us
    all_to_all x1, waiting for transfers between devices, per_device(): lax.all_to_all(kernel, 'filt', split_axis=3, concat_axis=2, tiled=True)  48.8 us
    all_gather x1, waiting for transfers between devices, per_device(): all_panels = lax.all_gather(rimmed, 'filt', axis=1, tiled=True)  39.7 us
    ppermute x4, starting transfers between devices, padded(): lax.ppermute(tail, axis, [(i, (i + 1) % count) for i in range(ends)])  16.2 us
    psum x1, blocking collectives, per_device(): lax.psum(lax.psum((kernel_part, bias_part), 'rep'), 'space')  13.3 us
    dot_general x9, matrix products, forward_taps(): jnp.einsum('oc,hcw->how', weights, window, preferred_element_type=jnp.flo...  11.2 us
    unnamed x23, local copies, waits for them, and re-layouts  11.1 us
    dot_general x9, matrix products, backward_taps(): jnp.einsum('oc,how->hcw', weights[row_tap, col_tap], part_slope, preferre...  8.55 us
  transfers between devices with their start and end apart: 13, of which 10 were waited for; matrix products, arithmetic and copies ran while one was open for 6% of the time, Pallas kernels for 0%

profile of v1, /device:TPU:0, one launch (start us, length us, event | category | flops | bytes accessed | tf_op | source)
XLA Modules:
  0.0 360.9 jit_solution(168119410281818128)
XLA Ops:
  7.2 1.5 copy.34
  8.7 1.3 collective-permute-start.1
  10.0 5.6 %collective-permute-start = (bf16[1,256,128]{1,2,0:T(8,128)(2,1)S(1)}, bf16[1,256,128]{1,2,0:T(8,128)(2,1)S(1)}, u32[]{:S(2)}, u32[]{:S(2)}) collective-permute-start(bf16[1,256,128]{1,2,0:T(8,128)(2,1)S(1)} %get-tuple-element.21), channel_id=1, source_target_pairs={{0,4},{4,8},{8,12},{1,5},{5,9},{9,13},{2,6},{6,10},{10,14},{3,7},{... | collective-permute-start | bytes 196616 | tf_op jit(solution)/shard_map/ppermute | solution.py:15
  15.6 0.3 collective-permute-done.1
  15.9 1.6 collective-permute-done
  17.6 1.4 collective-permute-start.3
  19.0 3.0 collective-permute-start.2
  22.0 0.8 collective-permute-done.2
  22.8 1.7 pad_maximum_fusion.1
  24.6 0.5 copy.38
  25.2 39.7 %all-gather.3.cloned.1.call-done = bf16[18,512,130]{1,2,0:T(8,128)(2,1)} async-done(((bf16[18,256,130]{1,2,0:T(8,128)(2,1)}), bf16[18,512,130]{1,2,0:T(8,128)(2,1)}) %all-gather.3.cloned.1.call-update) | async-done | bytes 2396176 | tf_op jit(solution)/shard_map/all_gather | solution.py:70
  64.9 2.5 fusion.33
  67.4 0.6 copy-done.2
  68.1 0.7 fusion.37
  68.8 0.8 fusion.41
  69.6 0.8 fusion.45
  70.3 0.7 fusion.49
  71.1 0.8 fusion.53
  71.8 0.8 fusion.57
  72.6 0.7 fusion.61
  73.4 3.4 convert_reduce_fusion
  76.8 0.8 fusion.91
  77.6 0.8 fusion.88
  78.3 0.7 fusion.85
  79.1 0.1 maximum_bitcast_fusion.2
  79.2 0.8 fusion.73
  80.0 0.8 fusion.70
  80.8 0.7 fusion.67
  81.5 0.8 fusion.82
  82.3 0.8 fusion.79
  83.0 0.7 fusion.76
  83.8 0.6 maximum_bitcast_fusion
  84.3 2.7 pad_maximum_fusion
  87.1 1.3 collective-permute-start.5
  88.4 4.5 %collective-permute-start.4 = (bf16[1,256,128]{1,2,0:T(8,128)(2,1)S(1)}, bf16[1,256,128]{1,2,0:T(8,128)(2,1)S(1)}, u32[]{:S(2)}, u32[]{:S(2)}) collective-permute-start(bf16[1,256,128]{1,2,0:T(8,128)(2,1)S(1)} %get-tuple-element.19), channel_id=1, source_target_pairs={{0,4},{4,8},{8,12},{1,5},{5,9},{9,13},{2,6},{6,10},{10,14},{3,7},{... | collective-permute-start | bytes 196616 | tf_op jit(solution)/shard_map/ppermute | solution.py:15
  93.0 0.3 collective-permute-done.5
  93.3 1.6 collective-permute-done.4
  94.9 1.6 collective-permute-start.7
  96.5 3.0 collective-permute-start.6
  99.5 0.8 collective-permute-done.6
  100.3 1.8 pad_maximum_fusion.2
  102.1 3.7 %copy.39 = bf16[3,3,256,512]{2,1,0,3:T(4,128)(2,1)} copy(bf16[3,3,256,512]{3,2,1,0:T(8,128)(2,1)S(1)} %copy-done.3) | data formatting | bytes 4718592 | tf_op args[1]
  105.9 4.2 %all-to-all-start = ((bf16[3,3,256,512]{2,1,0,3:T(4,128)(2,1)}), bf16[3,3,256,512]{2,1,0,3:T(4,128)(2,1)S(1)}, u32[]{:S(2)}, u32[]{:S(2)}) async-start(bf16[3,3,256,512]{2,1,0,3:T(4,128)(2,1)} %copy.39), calls=%async_computation | async-start | bytes 6291456 | tf_op jit(solution)/shard_map/all_to_all | solution.py:78
  110.2 6.0 %all-reduce.3.cloned.1.call-done = f32[3,3,256,512]{3,2,1,0:T(8,128)} async-done(((f32[3,3,256,512]{3,2,1,0:T(8,128)}), f32[3,3,256,512]{3,2,1,0:T(8,128)}) %all-reduce.3.cloned.1.call-update) | async-done | bytes 4718608 | tf_op jit(solution)/shard_map/psum | solution.py:82
  116.2 48.8 %all-to-all-done = bf16[3,3,256,512]{2,1,0,3:T(4,128)(2,1)S(1)} async-done(((bf16[3,3,256,512]{2,1,0,3:T(4,128)(2,1)}), bf16[3,3,256,512]{2,1,0,3:T(4,128)(2,1)S(1)}, u32[]{:S(2)}, u32[]{:S(2)}) %all-to-all-start) | async-done | bytes 2359328 | tf_op jit(solution)/shard_map/all_to_all | solution.py:78
  165.0 3.6 copy.40
  168.6 2.3 copy.59
  170.8 2.4 psum.30
  173.3 13.3 %psum.31 = f32[256]{0:T(256)S(1)} all-reduce(f32[256]{0:T(256)S(1)} %psum.30), channel_id=1, replica_groups=mesh['parts'=2,'space'=4,'filt'=2,'rep'=2] {'space'}, use_global_device_ids=true, to_apply=%region_4.0 | all-reduce | flops 256 | bytes 2048 | tf_op jit(solution)/shard_map/psum | solution.py:82
  186.6 0.6 broadcast_multiply_fusion.1
  187.2 2.5 fusion.5
  189.7 0.7 copy-done.4
  190.3 0.7 fusion.7
  191.1 0.7 fusion.9
  191.8 0.7 fusion.11
  192.5 0.7 fusion.13
  193.2 0.7 fusion.15
  193.9 0.7 fusion.19
  194.7 0.7 fusion.17
  195.4 0.5 copy-done.6
  195.9 1.1 fusion.2
  197.0 1.3 copy.60
  198.3 150.8 %all-reduce.5.cloned.1.call-done = f32[3,3,256,512]{3,2,1,0:T(8,128)} async-done(((f32[3,3,256,512]{3,2,1,0:T(8,128)}), f32[3,3,256,512]{3,2,1,0:T(8,128)}) %all-reduce.5.cloned.1.call-update) | async-done | bytes 4718608 | tf_op jit(solution)/shard_map/psum | solution.py:82
  349.1 5.3 %broadcast_multiply_fusion = f32[3,3,256,512]{3,2,1,0:T(8,128)} fusion(f32[3,3,256,512]{3,2,1,0:T(8,128)} %all-reduce.5.cloned.1.call-done), kind=kLoop, calls=%fused_computation.3 | loop fusion | flops 1179648 | bytes 9437184 | tf_op jit(solution)/shard_map/mul | solution.py:85
  (30 shorter events, 0.4 us)
Async XLA Ops:
  7.2 57.7 %all-gather.3.cloned.1.call-start = ((), (), s32[]{:S(2)}) async-start(), calls=%async_computation.1 | async-start | bytes 3760128 | tf_op jit(solution)/shard_map/all_gather | solution.py:70
  8.7 7.2 %collective-permute-start.1 = (bf16[1,256,128]{1,2,0:T(8,128)(2,1)S(1)}, bf16[1,256,128]{1,2,0:T(8,128)(2,1)S(1)}, u32[]{:S(2)}, u32[]{:S(2)}) collective-permute-start(bf16[1,256,128]{1,2,0:T(8,128)(2,1)S(1)} %get-tuple-element.22), channel_id=1, source_target_pairs={{4,0},{8,4},{12,8},{5,1},{9,5},{13,9},{6,2},{10,6},{14,10},{7,3},{... | collective-permute-start | bytes 196616 | tf_op jit(solution)/shard_map/ppermute | solution.py:17
  10.0 7.5 %collective-permute-start = (bf16[1,256,128]{1,2,0:T(8,128)(2,1)S(1)}, bf16[1,256,128]{1,2,0:T(8,128)(2,1)S(1)}, u32[]{:S(2)}, u32[]{:S(2)}) collective-permute-start(bf16[1,256,128]{1,2,0:T(8,128)(2,1)S(1)} %get-tuple-element.21), channel_id=1, source_target_pairs={{0,4},{4,8},{8,12},{1,5},{5,9},{9,13},{2,6},{6,10},{10,14},{3,7},{... | collective-permute-start | bytes 196616 | tf_op jit(solution)/shard_map/ppermute | solution.py:15
  17.5 7.1 %copy-start.7 = (bf16[16,256,128]{2,1,0:T(8,128)(2,1)S(1)}, bf16[16,256,128]{2,1,0:T(8,128)(2,1)}, u32[]{:S(2)}) copy-start(bf16[16,256,128]{2,1,0:T(8,128)(2,1)} %param.7) | copy-start | bytes 3145732
  17.6 4.5 %collective-permute-start.3 = (bf16[18,256,1]{1,2,0:T(2,128)(2,1)S(1)}, bf16[18,256,1]{1,2,0:T(2,128)(2,1)S(1)}, u32[]{:S(2)}, u32[]{:S(2)}) collective-permute-start(bf16[18,256,1]{1,2,0:T(2,128)(2,1)S(1)} %get-tuple-element.18), channel_id=1, source_target_pairs={{1,0},{3,2},{5,4},{7,6},{9,8},{11,10},{13,12},{15,14},{17,16},{19,... | collective-permute-start | bytes 27656 | tf_op jit(solution)/shard_map/ppermute | solution.py:17
  19.0 3.9 %collective-permute-start.2 = (bf16[18,256,1]{1,2,0:T(2,128)(2,1)S(1)}, bf16[18,256,1]{1,2,0:T(2,128)(2,1)S(1)}, u32[]{:S(2)}, u32[]{:S(2)}) collective-permute-start(bf16[18,256,1]{1,2,0:T(2,128)(2,1)S(1)} %get-tuple-element.17), channel_id=1, source_target_pairs={{0,1},{2,3},{4,5},{6,7},{8,9},{10,11},{12,13},{14,15},{16,17},{18,... | collective-permute-start | bytes 27656 | tf_op jit(solution)/shard_map/ppermute | solution.py:15
  24.6 91.5 %all-reduce.3.cloned.1.call-start = ((), (), s32[]{:S(2)}) async-start(), calls=%async_computation.3 | async-start | bytes 9437184 | tf_op jit(solution)/shard_map/psum | solution.py:82
  25.2 48.2 %copy-start.5 = (bf16[16,256,128]{1,2,0:T(8,128)(2,1)}, bf16[16,256,128]{1,2,0:T(8,128)(2,1)S(1)}, u32[]{:S(2)}) copy-start(bf16[16,256,128]{1,2,0:T(8,128)(2,1)S(1)} %copy.38) | copy-start | bytes 3145732
  64.9 2.5 copy-start
  64.9 3.2 copy-start.2
  72.6 0.8 copy-start.8
  87.1 100.1 %all-gather.5.cloned.1.call-start = ((), (), s32[]{:S(2)}) async-start(), calls=%async_computation.2 | async-start | bytes 3760128 | tf_op jit(solution)/shard_map/all_gather | solution.py:77
  87.1 6.2 %collective-permute-start.5 = (bf16[1,256,128]{1,2,0:T(8,128)(2,1)S(1)}, bf16[1,256,128]{1,2,0:T(8,128)(2,1)S(1)}, u32[]{:S(2)}, u32[]{:S(2)}) collective-permute-start(bf16[1,256,128]{1,2,0:T(8,128)(2,1)S(1)} %get-tuple-element.20), channel_id=1, source_target_pairs={{4,0},{8,4},{12,8},{5,1},{9,5},{13,9},{6,2},{10,6},{14,10},{7,3},{... | collective-permute-start | bytes 196616 | tf_op jit(solution)/shard_map/ppermute | solution.py:17
  88.4 6.4 %collective-permute-start.4 = (bf16[1,256,128]{1,2,0:T(8,128)(2,1)S(1)}, bf16[1,256,128]{1,2,0:T(8,128)(2,1)S(1)}, u32[]{:S(2)}, u32[]{:S(2)}) collective-permute-start(bf16[1,256,128]{1,2,0:T(8,128)(2,1)S(1)} %get-tuple-element.19), channel_id=1, source_target_pairs={{0,4},{4,8},{8,12},{1,5},{5,9},{9,13},{2,6},{6,10},{10,14},{3,7},{... | collective-permute-start | bytes 196616 | tf_op jit(solution)/shard_map/ppermute | solution.py:15
  94.9 7.2 %copy-start.3 = (bf16[3,3,256,512]{3,2,1,0:T(8,128)(2,1)S(1)}, bf16[3,3,256,512]{3,2,1,0:T(8,128)(2,1)}, u32[]{:S(2)}) copy-start(bf16[3,3,256,512]{3,2,1,0:T(8,128)(2,1)} %param.5) | copy-start | bytes 7077892
  94.9 4.6 %collective-permute-start.7 = (bf16[18,256,1]{1,2,0:T(2,128)(2,1)S(1)}, bf16[18,256,1]{1,2,0:T(2,128)(2,1)S(1)}, u32[]{:S(2)}, u32[]{:S(2)}) collective-permute-start(bf16[18,256,1]{1,2,0:T(2,128)(2,1)S(1)} %get-tuple-element.16), channel_id=1, source_target_pairs={{1,0},{3,2},{5,4},{7,6},{9,8},{11,10},{13,12},{15,14},{17,16},{19,... | collective-permute-start | bytes 27656 | tf_op jit(solution)/shard_map/ppermute | solution.py:17
  96.5 3.9 %collective-permute-start.6 = (bf16[18,256,1]{1,2,0:T(2,128)(2,1)S(1)}, bf16[18,256,1]{1,2,0:T(2,128)(2,1)S(1)}, u32[]{:S(2)}, u32[]{:S(2)}) collective-permute-start(bf16[18,256,1]{1,2,0:T(2,128)(2,1)S(1)} %get-tuple-element.15), channel_id=1, source_target_pairs={{0,1},{2,3},{4,5},{6,7},{8,9},{10,11},{12,13},{14,15},{16,17},{18,... | collective-permute-start | bytes 27656 | tf_op jit(solution)/shard_map/ppermute | solution.py:15
  105.9 59.1 %all-to-all-start = ((bf16[3,3,256,512]{2,1,0,3:T(4,128)(2,1)}), bf16[3,3,256,512]{2,1,0,3:T(4,128)(2,1)S(1)}, u32[]{:S(2)}, u32[]{:S(2)}) async-start(bf16[3,3,256,512]{2,1,0,3:T(4,128)(2,1)} %copy.39), calls=%async_computation | async-start | bytes 6291456 | tf_op jit(solution)/shard_map/all_to_all | solution.py:78
  110.1 239.0 %all-reduce.5.cloned.1.call-start = ((), (), s32[]{:S(2)}) async-start(), calls=%async_computation.4 | async-start | bytes 9437184 | tf_op jit(solution)/shard_map/psum | solution.py:82
  187.2 2.5 copy-start.1
  187.2 3.2 copy-start.4
  194.7 1.2 copy-start.6
Sparse Core Ops, SparseCore 0:
  24.7 40.1 all-gather.2
  87.2 28.9 all-reduce.2
  117.7 56.2 all-gather.4
  176.2 172.7 all-reduce.4
